TPU v7x, 128 devices: a whole 4x4x4 slice. The times are simulated.
128 devices in a mesh: sec: 16 (over y, z_lo, core), head: 8 (over z_hi, x).
Axes of the slice: x: 4, y: 4, z: 4 (z_hi: 2, z_lo: 2; z = z_hi * 2 + z_lo), core: 2. Of those that a mesh axis runs over, the one named last changes fastest.
Arguments:
- tokens: bfloat16 [16384, 4096], P('sec')
- w_query: bfloat16 [4096, 4096], P(None, 'head')
- w_key: bfloat16 [4096, 1024], P(None, 'head')
- w_value: bfloat16 [4096, 1024], P(None, 'head'), may hold values from -0.09375 to 0.09375
- w_out: bfloat16 [4096, 4096], P('head'), may hold values from -0.375 to 0.375
- key_start: int32 [64], replicated, may hold values from 0 to 16128, as said below
Outputs:
- mixed: bfloat16 [16384, 4096], P('sec', 'head')
Inputs may be any that keep to these rules, and one draw needn't show every extreme that they name: key_start[c] is a multiple of 256 and at most c * 256; the last block's entry is (64 - 1) * 256.
All inputs are finite; a program needn't handle non-finite values.
Results may differ from a plain program's by a relative error of at most 0.015.
The roundings to bfloat16 on the way count: a program that leaves them out, or rounds other values in their place, can miss the bound.
Values may be sent and summed in bfloat16 or wider, within the bound.
A program may use at most 128 MiB of HBM per device.

v0:
```python
import math
import jax
import jax.numpy as jnp
from jax import lax
from jax.sharding import PartitionSpec as P

QH = 32
KVH = 8
HD = 128
SPAN = 256


def rotate(heads_data, position):
    midway = heads_data.shape[-1] // 2
    frequency = jnp.float32(500000.0) ** (
        -(jnp.arange(midway, dtype=jnp.float32) * 2.0) / heads_data.shape[-1]
    )
    angle = position.astype(jnp.float32)[:, None] * frequency[None, :]
    cosine = jnp.cos(angle)[:, None, :]
    sine = jnp.sin(angle)[:, None, :]
    first_half = heads_data[..., :midway]
    second_half = heads_data[..., midway:]
    return jnp.concatenate(
        [first_half * cosine - second_half * sine, second_half * cosine + first_half * sine],
        axis=-1,
    )


def attend(query_sets, key_start, keys, values, local_groups, groups):
    table = jnp.arange(key_start.shape[0], dtype=jnp.int32)
    scale = HD ** (-0.5)
    prepared = []
    for queries, query_position in query_sets:
        number = queries.shape[0]
        span_index = query_position // SPAN
        lower = jnp.sum(
            jnp.where(span_index[:, None] == table[None, :], key_start[None, :], 0), axis=1
        )
        shaped = queries.reshape(number, local_groups, groups, HD)
        prepared.append((shaped, query_position, lower, jnp.min(lower), jnp.max(query_position)))
    shaped, query_position, lower, first_visible, last_query = prepared[0]
    number = shaped.shape[0]
    initial = [
        (
            jnp.full((local_groups, groups, number), -1e30, jnp.float32),
            jnp.zeros((local_groups, groups, number), jnp.float32),
            jnp.zeros((local_groups, groups, number, HD), jnp.float32),
        )
    ]
    key_piece = lax.all_gather(keys, "sec", axis=0, tiled=True)
    value_piece = lax.all_gather(values, "sec", axis=0, tiled=True)
    length = key_piece.shape[0]
    width = math.gcd(length, 1024)
    key_view = key_piece.reshape(length, local_groups, HD)
    value_view = value_piece.reshape(length, local_groups, HD)
    shaped, query_position, lower, first_visible, last_query = prepared[0]

    def one_block(
        index,
        state,
        shaped=shaped,
        query_position=query_position,
        lower=lower,
        first_visible=first_visible,
        last_query=last_query,
    ):
        offset = index * width

        def update(current):
            largest, weight_sum, gathered = current
            key_block = lax.dynamic_slice_in_dim(key_view, offset, width, 0)
            value_block = lax.dynamic_slice_in_dim(value_view, offset, width, 0)
            key_position = offset + jnp.arange(width, dtype=jnp.int32)
            scores = (
                jnp.einsum("qhgd,jhd->hgqj", shaped, key_block, preferred_element_type=jnp.float32)
                * scale
            )
            allowed = (key_position[None, :] >= lower[:, None]) & (
                key_position[None, :] <= query_position[:, None]
            )
            scores = jnp.where(allowed[None, None], scores, -jnp.inf)
            newest = jnp.maximum(largest, jnp.max(scores, axis=-1))
            weights = jnp.exp(scores - newest[..., None])
            factor = jnp.exp(largest - newest)
            weight_sum = weight_sum * factor + jnp.sum(weights, axis=-1)
            gathered = gathered * factor[..., None] + jnp.einsum(
                "hgqj,jhd->hgqd",
                weights.astype(jnp.bfloat16),
                value_block,
                preferred_element_type=jnp.float32,
            )
            return (newest, weight_sum, gathered)

        def keep_state(current):
            return current

        needed = (offset <= last_query) & (offset + width > first_visible)
        return lax.cond(needed, update, keep_state, state)

    updated = [lax.fori_loop(0, length // width, one_block, tuple(initial)[0])]
    states = tuple(updated)
    results = []
    for largest, weight_sum, gathered in states:
        number = gathered.shape[2]
        result = gathered / weight_sum[..., None]
        results.append(
            result.transpose(2, 0, 1, 3)
            .reshape(number, local_groups * groups * HD)
            .astype(jnp.bfloat16)
        )
    return results


def shards(tokens, w_query, w_key, w_value, w_out, key_start):
    rows = tokens.shape[0]
    local_groups = w_key.shape[1] // HD
    groups = QH // KVH
    section = lax.axis_index("sec")
    position = section * rows + jnp.arange(rows, dtype=jnp.int32)
    query = rotate(
        jnp.dot(tokens, w_query, preferred_element_type=jnp.float32).reshape(
            rows, local_groups * groups, HD
        ),
        position,
    )
    query = query.astype(jnp.bfloat16).reshape(rows, local_groups * groups * HD)
    keys = rotate(
        jnp.dot(tokens, w_key, preferred_element_type=jnp.float32).reshape(rows, local_groups, HD),
        position,
    )
    keys = keys.astype(jnp.bfloat16).reshape(rows, local_groups * HD)
    values = jnp.dot(tokens, w_value, preferred_element_type=jnp.float32).astype(jnp.bfloat16)
    attended = attend([(query, position)], key_start, keys, values, local_groups, groups)[0]
    terms = jnp.dot(attended, w_out, preferred_element_type=jnp.float32)
    mixed = lax.psum_scatter(terms.astype(jnp.bfloat16), "head", scatter_dimension=1, tiled=True)
    return mixed


def solution(mesh):
    placed = (
        P("sec", None),
        P(None, "head"),
        P(None, "head"),
        P(None, "head"),
        P("head", None),
        P(),
    )
    return jax.shard_map(
        shards, mesh=mesh, in_specs=placed, out_specs=P("sec", "head"), check_vma=False
    )
```

profile of v0, /device:TPU:0, one launch (start us, length us, event | category | flops | bytes accessed | tf_op | source)
XLA Modules:
  0.0 434.9 jit_solution(15608981831324070247)
XLA Ops:
  6.5 0.0 copy-start
  6.5 0.0 all-gather.3.cloned.1.call-start
  6.6 1.2 copy-done
  7.8 0.0 copy-start.3
  7.8 6.4 %convolution_bitcast_fusion = f32[1024,1,128]{0,2,1:T(8,128)S(1)} fusion(bf16[1024,4096]{1,0:T(8,128)(2,1)} %param.10, bf16[4096,128]{1,0:T(8,128)(2,1)S(1)} %copy-done), kind=kOutput, calls=%fused_computation.31 | convolution fusion | flops 1073741824 | bytes 9961472 | tf_op jit(solution)/shard_map/dot_general | solution.py:128
  14.1 1.2 fusion.33
  15.3 0.7 pad_maximum_fusion.1
  16.0 0.0 all-gather.3.cloned.1.call-update
  16.0 0.0 all-gather.5.cloned.1.call-start
  16.1 0.0 copy-done.3
  16.1 6.4 %convolution_convert_fusion.1 = bf16[1024,128]{1,0:T(8,128)(2,1)} fusion(bf16[1024,4096]{1,0:T(8,128)(2,1)} %param.10, bf16[4096,128]{1,0:T(8,128)(2,1)S(1)} %copy-done.3), kind=kOutput, calls=%fused_computation.32 | convolution fusion | flops 1073872896 | bytes 9699328 | tf_op jit(solution)/shard_map/dot_general | solution.py:132
  22.5 0.0 all-gather.5.cloned.1.call-update
  22.5 0.0 reduce-scatter.2.cloned.1.call-start
  22.6 8.3 %fusion.40 = f32[1024,512]{0,1:T(8,128)S(1)} fusion(bf16[1024,4096]{1,0:T(8,128)(2,1)} %param.10, bf16[4096,512]{1,0:T(8,128)(2,1)} %param.11), kind=kOutput, calls=%fused_computation.66 | convolution fusion | flops 4294967296 | bytes 14680064 | tf_op jit(solution)/shard_map/dot_general | solution.py:121
  30.8 1.2 fusion.39
  32.1 0.0 copy-start.2
  32.1 1.8 copy.23
  33.9 1.9 copy.22
  35.9 0.6 add_select_fusion
  36.5 0.0 copy-done.2
  36.5 0.1 select_reduce_fusion
  36.6 0.7 reduce_min.9
  37.3 1.9 multiply_cosine_fusion
  39.2 2.2 fusion.22
  41.3 0.6 pad_maximum_fusion
  41.9 14.0 %all-gather.3.cloned.1.call-done = bf16[16384,128]{0,1:T(8,128)(2,1)} async-done(((bf16[1024,128]{0,1:T(8,128)(2,1)}), bf16[16384,128]{0,1:T(8,128)(2,1)}) %all-gather.3.cloned.1.call-update) | async-done | bytes 4194320 | tf_op jit(solution)/shard_map/all_gather | solution.py:50
  55.9 6.4 %copy.19 = bf16[16384,1,128]{2,0,1:T(8,128)(2,1)} copy(bf16[16384,1,128]{0,2,1:T(8,128)(2,1)} %bitcast.72) | data formatting | bytes 8388608
  62.3 32.7 %all-gather.5.cloned.1.call-done = bf16[16384,128]{1,0:T(8,128)(2,1)} async-done(((bf16[1024,128]{1,0:T(8,128)(2,1)}), bf16[16384,128]{1,0:T(8,128)(2,1)}) %all-gather.5.cloned.1.call-update) | async-done | bytes 4194320 | tf_op jit(solution)/shard_map/all_gather | solution.py:51
  95.0 0.1 broadcast_in_dim.28
  95.2 35.4 %while.18 = (s32[]{:T(128)}, f32[1,4,1024]{2,1,0:T(4,128)S(1)}, f32[1,4,1024]{2,1,0:T(4,128)S(1)}, f32[1,4,1024,128]{3,2,1,0:T(8,128)S(1)}, s32[]{:T(128)}, /*in...) while((s32[]{:T(128)}, f32[1,4,1024]{2,1,0:T(4,128)S(1)}, ...), condition=%wide.region_8.9_spmd.clone, body=%wide.region_3.8_spmd.clone.sunk | while | flops 2197829632 | bytes 60584296 | solution.py:100
  96.7 14.2 %conditional.3 = ((f32[1,4,1024]{2,1,0:T(4,128)S(1)}, f32[1,4,1024]{2,1,0:T(4,128)S(1)}, f32[1,4,1024,128]{3,2,1,0:T(8,128)S(1)})) conditional(s32[]{:T(128)} %convert_element_type.63, (f32[1,4,1024]{2,1,0:T(4,128)S(1)}, f32[1,4,1024]{2,1,0:T(4,128)S(1)}, f32[1,4,1024,128]{3,2,1,0:T(8,128)S(1)}) %tuple.53, (s32[]{:T(128)}, s32[1024]{0:T(1024)S(1)}, ...), branch_computations={%region_4.4_spmd, %region_5.7_spmd} | conditional | flops 2197829632 | bytes 60579924 | solution.py:98
  96.7 0.9 compare_and_fusion
  97.6 3.8 fusion.4
  101.4 5.8 %bitcast_add_fusion = f32[1,4,1024,128]{3,2,1,0:T(8,128)S(1)} fusion(f32[1,4,1024,128]{3,2,1,0:T(8,128)S(1)} %get-tuple-element.213, f32[1024,1024,4]{1,0,2:T(8,128)S(1)} %get-tuple-element.323, f32[4,1024]{1,0:T(4,128)S(1)} %bitcast.70, pred[1024,1024]{0,1:T(8,128)(4,1)S(1)} %compare_and_fusion, f32[4,1024]{1,0:T(4,128)S(1)} %get-tuple-element.320, ...), kind=kOutput, calls=%fused_computation.10 | convolution fusion | flops 1091567616 | bytes 22315012 | tf_op jit(solution)/shard_map/while/body/eval_jaxpr/cond/branch_1_fun/hgqj,jhd->hgqd/dot_general | solution.py:86
  107.2 3.7 fusion.3
  130.6 1.9 copy.20
  132.4 1.8 divide_convert_fusion
  134.3 9.0 %convolution_convert_fusion = bf16[1024,4096]{1,0:T(8,128)(2,1)} fusion(bf16[1024,512]{0,1:T(8,128)(2,1)S(1)} %bitcast.74, bf16[512,4096]{1,0:T(8,128)(2,1)} %param.14), kind=kOutput, calls=%fused_computation.27 | convolution fusion | flops 4299161600 | bytes 13631488 | tf_op jit(solution)/shard_map/dot_general | solution.py:134
  143.3 0.0 copy-start.1
  143.3 0.0 reduce-scatter.2.cloned.1.call-update
  143.3 285.1 %reduce-scatter.2.cloned.1.call-done = bf16[1024,512]{1,0:T(8,128)(2,1)} async-done(((bf16[1024,4096]{1,0:T(8,128)(2,1)}), bf16[1024,512]{1,0:T(8,128)(2,1)}) %reduce-scatter.2.cloned.1.call-update) | async-done | bytes 1048592 | tf_op jit(solution)/shard_map/reduce_scatter | solution.py:135
  428.4 0.0 copy-done.1
  (39 shorter events, 0.4 us)
Async XLA Ops:
  6.5 1.2 copy-start
  6.5 49.4 %all-gather.3.cloned.1.call-start = ((), (), s32[]{:S(2)}) async-start(), calls=%async_computation.1 | async-start | bytes 4456448 | tf_op jit(solution)/shard_map/all_gather | solution.py:50
  7.8 8.3 %copy-start.3 = (bf16[4096,128]{1,0:T(8,128)(2,1)S(1)}, bf16[4096,128]{1,0:T(8,128)(2,1)}, u32[]{:S(2)}) copy-start(bf16[4096,128]{1,0:T(8,128)(2,1)} %param.13) | copy-start | bytes 3145732
  16.0 79.0 %all-gather.5.cloned.1.call-start = ((), (), s32[]{:S(2)}) async-start(), calls=%async_computation.2 | async-start | bytes 4456448 | tf_op jit(solution)/shard_map/all_gather | solution.py:51
  22.5 405.8 %reduce-scatter.2.cloned.1.call-start = ((), (), s32[]{:S(2)}) async-start(), calls=%async_computation.3 | async-start | bytes 9437184 | tf_op jit(solution)/shard_map/reduce_scatter | solution.py:135
  32.1 4.4 %copy-start.2 = (s32[64]{0:T(128)S(1)}, s32[64]{0:T(128)}, u32[]{:S(2)}) copy-start(s32[64]{0:T(128)} %param.15) | copy-start | bytes 772
  143.3 285.1 %copy-start.1 = (bf16[4096,128]{1,0:T(8,128)(2,1)S(1)}, bf16[4096,128]{1,0:T(8,128)(2,1)}, u32[]{:S(2)}) copy-start(bf16[4096,128]{1,0:T(8,128)(2,1)} %param.12) | copy-start | bytes 3145732
Sparse Core Ops, SparseCore 0:
  16.2 39.6 all-gather.2
  57.6 37.3 all-gather.4
  143.4 284.9 reduce-scatter.1
where the time goes:
time: 436 us; the launch traced here: 435 us
  waiting for transfers between devices  332 us (76%)
  matrix products  39.6 us (9%)
  loops' own time  21.2 us (5%)
  local copies, waits for them, and re-layouts  14.7 us (3%)
  other arithmetic  14.3 us (3%)
  between operations  13.2 us (3%)
    reduce_scatter x1, waiting for transfers between devices, shards(): lax.psum_scatter(terms.astype(jnp.bfloat16), 'head', scatter_dimension=1,...  285 us
    all_gather x1, waiting for transfers between devices, attend(): value_piece = lax.all_gather(values, 'sec', axis=0, tiled=True)  32.7 us
    another operation x1, loops' own time, attend(): updated = [lax.fori_loop(0, length // width, one_block, tuple(initial)[0])]  20.9 us
    all_gather x1, waiting for transfers between devices, attend(): key_piece = lax.all_gather(keys, 'sec', axis=0, tiled=True)  14 us
    unnamed x11, local copies, waits for them, and re-layouts  11.4 us
    dot_general x1, matrix products, shards(): terms = jnp.dot(attended, w_out, preferred_element_type=jnp.float32)  8.97 us
  transfers between devices with their start and end apart: 3, of which 3 were waited for; matrix products, arithmetic and copies ran while one was open for 7% of the time, Pallas kernels for 0%

commit v1 on v0

--- a/solution.py
+++ b/solution.py
@@ -48,7 +48,10 @@
         )
     ]
     key_piece = lax.all_gather(keys, "sec", axis=0, tiled=True)
-    value_piece = lax.all_gather(values, "sec", axis=0, tiled=True)
+    size = lax.axis_size("sec")
+    blocks = jnp.stack([values for _ in range(size)])
+    blocks = lax.all_to_all(blocks, "sec", split_axis=0, concat_axis=0)
+    value_piece = jnp.concatenate(blocks, axis=0)
     length = key_piece.shape[0]
     width = math.gcd(length, 1024)
     key_view = key_piece.reshape(length, local_groups, HD)

time: 436 us -> 451 us (1.034)
  starting transfers between devices: 0.09 us -> 6.31 us
    all_gather x1 -> x0, waiting for transfers between devices: 32.7 us -> none  [attend(): value_piece = lax.all_gather(values, 'sec', axis=0, tiled=True)]
    all_gather x1, waiting for transfers between devices: 14 us -> 46.3 us  [attend(): key_piece = lax.all_gather(keys, 'sec', axis=0, tiled=True)]
    all_to_all x0 -> x1, starting transfers between devices: none -> 6.09 us  [attend(): blocks = lax.all_to_all(blocks, 'sec', split_axis=0, concat_axis=0)]
    reduce_scatter x1, waiting for transfers between devices: 285 us -> 290 us  [shards(): lax.psum_scatter(terms.astype(jnp.bfloat16), 'head', scatter_dimension=1,...]
  transfers between devices with their start and end apart: 3 -> 3, of which waited for: 3 -> 2; matrix products, arithmetic and copies ran while one was open for 7% -> 8% of each run, Pallas kernels for 0% -> 0%
where the time goes in v1:
time: 451 us; the launch traced here: 449 us
  waiting for transfers between devices  336 us (75%)
  matrix products  39 us (9%)
  loops' own time  22.5 us (5%)
  local copies, waits for them, and re-layouts  17.4 us (4%)
  other arithmetic  14.3 us (3%)
  between operations  13.5 us (3%)
  starting transfers between devices  6.31 us (1%)
    reduce_scatter x1, waiting for transfers between devices, shards(): lax.psum_scatter(terms.astype(jnp.bfloat16), 'head', scatter_dimension=1,...  290 us
    all_gather x1, waiting for transfers between devices, attend(): key_piece = lax.all_gather(keys, 'sec', axis=0, tiled=True)  46.3 us
    another operation x1, loops' own time, attend(): updated = [lax.fori_loop(0, length // width, one_block, tuple(initial)[0])]  22.2 us
    unnamed x11, local copies, waits for them, and re-layouts  11.4 us
  transfers between devices with their start and end apart: 3, of which 2 were waited for; matrix products, arithmetic and copies ran while one was open for 8% of the time, Pallas kernels for 0%

profile of v1, /device:TPU:0, one launch (start us, length us, event | category | flops | bytes accessed | tf_op | source)
XLA Modules:
  0.0 449.2 jit_solution(6983356513757046712)
XLA Ops:
  6.5 0.0 copy-start
  6.5 0.0 all-gather.2.cloned.1.call-start
  6.6 1.2 copy-done
  7.8 0.0 copy-start.3
  7.8 6.4 %convolution_bitcast_fusion = f32[1024,1,128]{0,2,1:T(8,128)S(1)} fusion(bf16[1024,4096]{1,0:T(8,128)(2,1)} %param.10, bf16[4096,128]{1,0:T(8,128)(2,1)S(1)} %copy-done), kind=kOutput, calls=%fused_computation.31 | convolution fusion | flops 1073741824 | bytes 9961472 | tf_op jit(solution)/shard_map/dot_general | solution.py:131
  14.1 1.2 fusion.33
  15.3 0.7 pad_maximum_fusion.1
  16.0 0.0 all-gather.2.cloned.1.call-update
  16.0 0.0 copy-done.3
  16.0 5.7 %convolution_convert_fusion.1 = bf16[1024,128]{1,0:T(8,128)(2,1)S(1)} fusion(bf16[1024,4096]{1,0:T(8,128)(2,1)} %param.10, bf16[4096,128]{1,0:T(8,128)(2,1)S(1)} %copy-done.3), kind=kOutput, calls=%fused_computation.32 | convolution fusion | flops 1073872896 | bytes 9699328 | tf_op jit(solution)/shard_map/dot_general | solution.py:135
  21.8 2.8 stack.2
  24.5 6.1 %all-to-all-start = ((bf16[16,1024,128]{2,1,0:T(8,128)(2,1)}), bf16[16,1024,128]{2,1,0:T(8,128)(2,1)}, u32[]{:S(2)}, u32[]{:S(2)}) async-start(bf16[16,1024,128]{2,1,0:T(8,128)(2,1)} %stack.2), calls=%async_computation | async-start | bytes 8388608 | tf_op jit(solution)/shard_map/all_to_all | solution.py:53
  30.6 0.2 reduce-scatter.2.cloned.1.call-start
  30.8 8.4 %fusion.40 = f32[1024,512]{0,1:T(8,128)S(1)} fusion(bf16[1024,4096]{1,0:T(8,128)(2,1)} %param.10, bf16[4096,512]{1,0:T(8,128)(2,1)} %param.11), kind=kOutput, calls=%fused_computation.66 | convolution fusion | flops 4294967296 | bytes 14680064 | tf_op jit(solution)/shard_map/dot_general | solution.py:124
  39.3 1.2 fusion.39
  40.5 0.0 copy-start.2
  40.5 1.8 copy.23
  42.3 1.9 copy.22
  44.3 0.6 add_select_fusion
  44.9 0.0 copy-done.2
  44.9 0.1 select_reduce_fusion
  45.0 0.7 reduce_min.9
  45.7 1.9 multiply_cosine_fusion
  47.6 2.1 fusion.22
  49.7 0.6 pad_maximum_fusion
  50.3 46.3 %all-gather.2.cloned.1.call-done = bf16[16384,128]{0,1:T(8,128)(2,1)} async-done(((bf16[1024,128]{0,1:T(8,128)(2,1)}), bf16[16384,128]{0,1:T(8,128)(2,1)}) %all-gather.2.cloned.1.call-update) | async-done | bytes 4194320 | tf_op jit(solution)/shard_map/all_gather | solution.py:50
  96.6 6.4 %copy.19 = bf16[16384,1,128]{2,0,1:T(8,128)(2,1)} copy(bf16[16384,1,128]{0,2,1:T(8,128)(2,1)} %bitcast.72) | data formatting | bytes 8388608
  103.1 0.0 all-to-all-done
  103.1 0.1 broadcast_in_dim.28
  103.2 36.7 %while.18 = (s32[]{:T(128)}, f32[1,4,1024]{2,1,0:T(4,128)S(1)}, f32[1,4,1024]{2,1,0:T(4,128)S(1)}, f32[1,4,1024,128]{3,2,1,0:T(8,128)S(1)}, s32[]{:T(128)}, /*in...) while((s32[]{:T(128)}, f32[1,4,1024]{2,1,0:T(4,128)S(1)}, ...), condition=%wide.region_8.9_spmd.clone, body=%wide.region_3.8_spmd.clone.sunk | while | flops 2197829632 | bytes 60584296 | solution.py:103
  104.8 14.2 %conditional.3 = ((f32[1,4,1024]{2,1,0:T(4,128)S(1)}, f32[1,4,1024]{2,1,0:T(4,128)S(1)}, f32[1,4,1024,128]{3,2,1,0:T(8,128)S(1)})) conditional(s32[]{:T(128)} %convert_element_type.63, (f32[1,4,1024]{2,1,0:T(4,128)S(1)}, f32[1,4,1024]{2,1,0:T(4,128)S(1)}, f32[1,4,1024,128]{3,2,1,0:T(8,128)S(1)}) %tuple.53, (s32[]{:T(128)}, s32[1024]{0:T(1024)S(1)}, ...), branch_computations={%region_4.4_spmd, %region_5.7_spmd} | conditional | flops 2197829632 | bytes 60579924 | solution.py:101
  104.8 0.9 compare_and_fusion
  105.7 3.8 fusion.4
  109.6 5.8 %bitcast_add_fusion = f32[1,4,1024,128]{3,2,1,0:T(8,128)S(1)} fusion(f32[1,4,1024,128]{3,2,1,0:T(8,128)S(1)} %get-tuple-element.213, f32[1024,1024,4]{1,0,2:T(8,128)S(1)} %get-tuple-element.323, f32[4,1024]{1,0:T(4,128)S(1)} %bitcast.70, pred[1024,1024]{0,1:T(8,128)(4,1)S(1)} %compare_and_fusion, f32[4,1024]{1,0:T(4,128)S(1)} %get-tuple-element.320, ...), kind=kOutput, calls=%fused_computation.10 | convolution fusion | flops 1091567616 | bytes 22315012 | tf_op jit(solution)/shard_map/while/body/eval_jaxpr/cond/branch_1_fun/hgqj,jhd->hgqd/dot_general | solution.py:89
  115.3 3.7 fusion.3
  139.9 1.9 copy.20
  141.8 1.8 divide_convert_fusion
  143.7 9.0 %convolution_convert_fusion = bf16[1024,4096]{1,0:T(8,128)(2,1)} fusion(bf16[1024,512]{0,1:T(8,128)(2,1)S(1)} %bitcast.74, bf16[512,4096]{1,0:T(8,128)(2,1)} %param.14), kind=kOutput, calls=%fused_computation.27 | convolution fusion | flops 4299161600 | bytes 13631488 | tf_op jit(solution)/shard_map/dot_general | solution.py:137
  152.6 0.0 copy-start.1
  152.6 0.0 reduce-scatter.2.cloned.1.call-update
  152.7 289.7 %reduce-scatter.2.cloned.1.call-done = bf16[1024,512]{1,0:T(8,128)(2,1)} async-done(((bf16[1024,4096]{1,0:T(8,128)(2,1)}), bf16[1024,512]{1,0:T(8,128)(2,1)}) %reduce-scatter.2.cloned.1.call-update) | async-done | bytes 1048592 | tf_op jit(solution)/shard_map/reduce_scatter | solution.py:138
  442.4 0.0 copy-done.1
  (39 shorter events, 0.4 us)
Async XLA Ops:
  6.5 1.2 copy-start
  6.5 90.1 %all-gather.2.cloned.1.call-start = ((), (), s32[]{:S(2)}) async-start(), calls=%async_computation.2 | async-start | bytes 4456448 | tf_op jit(solution)/shard_map/all_gather | solution.py:50
  7.8 8.3 %copy-start.3 = (bf16[4096,128]{1,0:T(8,128)(2,1)S(1)}, bf16[4096,128]{1,0:T(8,128)(2,1)}, u32[]{:S(2)}) copy-start(bf16[4096,128]{1,0:T(8,128)(2,1)} %param.13) | copy-start | bytes 3145732
  24.5 78.5 %all-to-all-start = ((bf16[16,1024,128]{2,1,0:T(8,128)(2,1)}), bf16[16,1024,128]{2,1,0:T(8,128)(2,1)}, u32[]{:S(2)}, u32[]{:S(2)}) async-start(bf16[16,1024,128]{2,1,0:T(8,128)(2,1)} %stack.2), calls=%async_computation | async-start | bytes 8388608 | tf_op jit(solution)/shard_map/all_to_all | solution.py:53
  30.6 411.8 %reduce-scatter.2.cloned.1.call-start = ((), (), s32[]{:S(2)}) async-start(), calls=%async_computation.3 | async-start | bytes 9437184 | tf_op jit(solution)/shard_map/reduce_scatter | solution.py:138
  40.5 4.4 copy-start.2
  152.6 289.7 %copy-start.1 = (bf16[4096,128]{1,0:T(8,128)(2,1)S(1)}, bf16[4096,128]{1,0:T(8,128)(2,1)}, u32[]{:S(2)}) copy-start(bf16[4096,128]{1,0:T(8,128)(2,1)} %param.12) | copy-start | bytes 3145732
Sparse Core Ops, SparseCore 0:
  16.2 80.4 all-gather.1
  152.8 289.5 reduce-scatter.1
